TPU v7x, 32 devices: a whole 2x2x4 slice. The times are simulated.
32 devices in a mesh: dp: 8 (over y, x, core), tensor: 4 (over z).
Axes of the slice: x: 2, y: 2, z: 4, core: 2. Of those that a mesh axis runs over, the one named last changes fastest.
Arguments:
- tokens: bfloat16 [8192, 2048], P('dp'), may hold values from -6 to 6
- cotangent: bfloat16 [8192, 2048], P('dp'), may hold values from -6 to 6
- segment_ids: int32 [8, 1024], P('dp'), may hold values from 0 to 2, never falling along the last dimension, each value on 1 to 768 neighbouring positions
- step_count: int32 [1], replicated, may hold values from 2 to 4
- norm_gains: float32 [2, 2048], P(None, 'dp'), may hold values from 0.5 to 1.5
- gains_first: float32 [2, 2048], P(None, 'dp'), may hold values from -0.0004272461 to 0.0004272461
- gains_second: float32 [2, 2048], P(None, 'dp'), may hold values from 9.5358565e-09 to 1.5211961e-07
- w_query: float32 [2048, 2048], P('dp', 'tensor'), may hold values from -0.125 to 0.125
- query_first: float32 [2048, 2048], P('dp', 'tensor'), may hold values from -0.00015258789 to 0.00015258789
- query_second: float32 [2048, 2048], P('dp', 'tensor'), may hold values from 1.4757873e-09 to 2.3839641e-08
- w_keyval: float32 [2, 2048, 256], P(None, 'dp', 'tensor'), may hold values from -0.125 to 0.125
- keyval_first: float32 [2, 2048, 256], P(None, 'dp', 'tensor'), may hold values from -0.0004272461 to 0.0004272461
- keyval_second: float32 [2, 2048, 256], P(None, 'dp', 'tensor'), may hold values from 1.0353215e-08 to 1.6710453e-07
- w_out: float32 [2048, 2048], P('tensor', 'dp'), may hold values from -1.5 to 1.5
- out_first: float32 [2048, 2048], P('tensor', 'dp'), may hold values from -1.5258789e-05 to 1.5258789e-05
- out_second: float32 [2048, 2048], P('tensor', 'dp'), may hold values from 1.7709447e-11 to 2.860757e-10
- w_gateup: float32 [2, 2048, 5632], P(None, 'dp', 'tensor'), may hold values from -0.125 to 0.125
- gateup_first: float32 [2, 2048, 5632], P(None, 'dp', 'tensor'), may hold values from -5.340576e-05 to 5.340576e-05
- gateup_second: float32 [2, 2048, 5632], P(None, 'dp', 'tensor'), may hold values from 1.4757873e-10 to 2.3839641e-09
- w_down: float32 [5632, 2048], P('tensor', 'dp'), may hold values from -0.15625 to 0.15625
- down_first: float32 [5632, 2048], P('tensor', 'dp'), may hold values from -4.5776367e-05 to 4.5776367e-05
- down_second: float32 [5632, 2048], P('tensor', 'dp'), may hold values from 1.1806298e-10 to 1.9071713e-09
Outputs:
- layer_out: bfloat16 [8192, 2048], P('dp')
- input_grad: float32 [8192, 2048], P('dp')
- grad_norm: float32 [1], replicated
- gains_moment: float32 [2, 2048], P(None, 'dp')
- gains_square: float32 [2, 2048], P(None, 'dp')
- gains_new: float32 [2, 2048], P(None, 'dp')
- query_moment: float32 [2048, 2048], P('dp', 'tensor')
- query_square: float32 [2048, 2048], P('dp', 'tensor')
- query_new: float32 [2048, 2048], P('dp', 'tensor')
- keyval_moment: float32 [2, 2048, 256], P(None, 'dp', 'tensor')
- keyval_square: float32 [2, 2048, 256], P(None, 'dp', 'tensor')
- keyval_new: float32 [2, 2048, 256], P(None, 'dp', 'tensor')
- out_moment: float32 [2048, 2048], P('tensor', 'dp')
- out_square: float32 [2048, 2048], P('tensor', 'dp')
- out_new: float32 [2048, 2048], P('tensor', 'dp')
- gateup_moment: float32 [2, 2048, 5632], P(None, 'dp', 'tensor')
- gateup_square: float32 [2, 2048, 5632], P(None, 'dp', 'tensor')
- gateup_new: float32 [2, 2048, 5632], P(None, 'dp', 'tensor')
- down_moment: float32 [5632, 2048], P('tensor', 'dp')
- down_square: float32 [5632, 2048], P('tensor', 'dp')
- down_new: float32 [5632, 2048], P('tensor', 'dp')
Inputs may be any that keep to these rules, and one draw needn't show every extreme that they name: `segment_ids`: in each batch row the segment ids never fall, all 3 ids occur, and the longest sequence of a row has 768 tokens; a token attends to the earlier tokens of its own sequence only.
All inputs are finite; a program needn't handle non-finite values.
Results may differ from a plain program's by a relative error of at most 0.017.
Values may be sent and summed in bfloat16 or wider, within the bound.
A program may use at most 320 MiB of HBM per device.

v0:
```python
import jax
import jax.numpy as jnp
from jax import lax
from jax.sharding import PartitionSpec as P

HD = 64
norm_eps = 1e-05
beta_first = 0.9
beta_second = 0.95
adam_eps = 1e-08
weight_decay = 0.1
weight_rate = 0.02
out_rate = 0.1
gain_rate = 0.2
clip_limit = 1.0
masked_value = -1000000000.0


def positions(segment):
    length = segment.shape[0]
    indices = jnp.arange(length, dtype=jnp.int32)
    earlier = jnp.concatenate([segment[:1] - 1, segment[:-1]])
    begins = jnp.where(segment != earlier, indices, jnp.zeros_like(indices))
    return indices - lax.cummax(begins, axis=0)


def rotary_tables(places, width):
    half_width = width // 2
    frequency = jnp.power(10000.0, -jnp.arange(half_width, dtype=jnp.float32) * (2.0 / width))
    angles = places.astype(jnp.float32)[:, None] * frequency[None, :]
    cosine_table = jnp.concatenate([jnp.cos(angles), jnp.cos(angles)], axis=-1)
    sine_table = jnp.concatenate([jnp.sin(angles), jnp.sin(angles)], axis=-1)
    return (cosine_table, sine_table)


def rotate(values, cosine_table, sine_table):
    half_width = values.shape[-1] // 2
    turned = jnp.concatenate([-values[..., half_width:], values[..., :half_width]], axis=-1)
    return values * cosine_table[:, None, :] + turned * sine_table[:, None, :]


def unrotate(gradient, cosine_table, sine_table):
    half_width = gradient.shape[-1] // 2
    along_sine = gradient * sine_table[:, None, :]
    turned = jnp.concatenate([along_sine[..., half_width:], -along_sine[..., :half_width]], axis=-1)
    return gradient * cosine_table[:, None, :] + turned


def over_rows(left, right):
    return lax.dot_general(
        left, right, (((0,), (0,)), ((), ())), preferred_element_type=jnp.float32
    )


def against(left, right):
    return lax.dot_general(
        left, right, (((1,), (1,)), ((), ())), preferred_element_type=jnp.float32
    )


def norm_back(grad_output, unit_rows, inverse, gain):
    scaled = grad_output * gain
    gain_grad = jnp.sum(grad_output * unit_rows, axis=0)
    inner_mean = jnp.mean(scaled * unit_rows, axis=-1, keepdims=True)
    return (inverse * (scaled - unit_rows * inner_mean), gain_grad)


def adam_step(weight, first, second, gradient, clip_factor, step_float, step_rate, decay_rate):
    gradient = gradient * clip_factor
    first = beta_first * first + (1.0 - beta_first) * gradient
    second = beta_second * second + (1.0 - beta_second) * gradient * gradient
    correct_one = 1.0 - jnp.power(beta_first, step_float)
    correct_two = 1.0 - jnp.power(beta_second, step_float)
    update = first / correct_one / (jnp.sqrt(second / correct_two) + adam_eps)
    return (first, second, weight - step_rate * (update + decay_rate * weight))


def on_device(
    tokens,
    cotangent,
    segment_ids,
    step_count,
    norm_gains,
    gains_first,
    gains_second,
    w_query,
    query_first,
    query_second,
    w_keyval,
    keyval_first,
    keyval_second,
    w_out,
    out_first,
    out_second,
    w_gateup,
    gateup_first,
    gateup_second,
    w_down,
    down_first,
    down_second,
):
    gathered = (
        lax.all_gather(norm_gains.astype(jnp.bfloat16), "dp", axis=1, tiled=True),
        lax.all_gather(w_query.astype(jnp.bfloat16), "dp", axis=0, tiled=True),
        lax.all_gather(w_keyval.astype(jnp.bfloat16), "dp", axis=1, tiled=True),
        lax.all_gather(w_out.astype(jnp.bfloat16), "dp", axis=1, tiled=True),
        lax.all_gather(w_gateup.astype(jnp.bfloat16), "dp", axis=1, tiled=True),
        lax.all_gather(w_down.astype(jnp.bfloat16), "dp", axis=1, tiled=True),
    )
    gain_rows, query_weight, keyval_weight, out_weight, gateup_weight, down_weight = gathered
    gain_values = gain_rows.astype(jnp.float32)
    length = tokens.shape[0]
    segment = segment_ids[0]
    local_heads = query_weight.shape[1] // HD
    local_groups = keyval_weight.shape[2] // HD
    group_size = local_heads // local_groups
    cosine_table, sine_table = rotary_tables(positions(segment), HD)
    indices = jnp.arange(length, dtype=jnp.int32)
    block_rows = min(512, length)
    starts = jnp.arange(length // block_rows, dtype=jnp.int32) * block_rows
    inverse_scale = HD ** (-0.5)
    values_in = tokens.astype(jnp.float32)
    inverse_one = lax.rsqrt(jnp.mean(values_in * values_in, axis=-1, keepdims=True) + norm_eps)
    unit_one = values_in * inverse_one
    normed_one = (unit_one * gain_values[0]).astype(jnp.bfloat16)
    query_raw = jnp.dot(normed_one, query_weight, preferred_element_type=jnp.float32)
    queries = rotate(query_raw.reshape(length, local_heads, HD), cosine_table, sine_table).astype(
        jnp.bfloat16
    )
    queries = queries.reshape(length, local_groups, group_size, HD)
    keyval_raw = jnp.einsum(
        "nd,sdk->snk", normed_one, keyval_weight, preferred_element_type=jnp.float32
    )
    key_rows = rotate(
        keyval_raw[0].reshape(length, local_groups, HD), cosine_table, sine_table
    ).astype(jnp.bfloat16)
    value_rows = keyval_raw[1].reshape(length, local_groups, HD).astype(jnp.bfloat16)

    def block_scores(start):
        query_block = lax.dynamic_slice_in_dim(queries, start, block_rows, 0)
        segment_block = lax.dynamic_slice_in_dim(segment, start, block_rows, 0)
        row_index = start + jnp.arange(block_rows, dtype=jnp.int32)
        allowed = (segment_block[:, None] == segment[None, :]) & (
            row_index[:, None] >= indices[None, :]
        )
        raw_scores = jnp.einsum(
            "qkgh,pkh->kgqp", query_block, key_rows, preferred_element_type=jnp.float32
        )
        return (query_block, jnp.where(allowed, raw_scores * inverse_scale, masked_value))

    def forward_block(start):
        query_block, scaled = block_scores(start)
        highest = jnp.max(scaled, axis=-1, keepdims=True)
        lifted = jnp.exp(scaled - highest)
        row_total = jnp.sum(lifted, axis=-1, keepdims=True)
        soft_weights = (lifted / row_total).astype(jnp.bfloat16)
        mixed = jnp.einsum(
            "kgqp,pkh->qkgh", soft_weights, value_rows, preferred_element_type=jnp.float32
        )
        return (
            mixed.astype(jnp.bfloat16).reshape(block_rows, local_heads * HD),
            (highest + jnp.log(row_total))[..., 0],
        )

    mixed_blocks, logsum_blocks = lax.map(forward_block, starts)
    mixture = mixed_blocks.reshape(length, local_heads * HD)
    branch_partial = jnp.dot(mixture, out_weight, preferred_element_type=jnp.float32)
    branch = lax.psum(branch_partial, "tensor")
    middle = values_in + branch
    inverse_two = lax.rsqrt(jnp.mean(middle * middle, axis=-1, keepdims=True) + norm_eps)
    unit_two = middle * inverse_two
    normed_two = (unit_two * gain_values[1]).astype(jnp.bfloat16)
    gateup = jnp.einsum(
        "nd,sdf->snf", normed_two, gateup_weight, preferred_element_type=jnp.float32
    )
    hidden = (jax.nn.silu(gateup[0]) * gateup[1]).astype(jnp.bfloat16)
    feed_out = lax.psum(
        jnp.dot(hidden, down_weight, preferred_element_type=jnp.float32).astype(jnp.bfloat16),
        "tensor",
    ).astype(jnp.float32)
    layer_out = (middle + feed_out).astype(jnp.bfloat16)
    regathered = (
        lax.all_gather(norm_gains.astype(jnp.bfloat16), "dp", axis=1, tiled=True),
        lax.all_gather(w_query.astype(jnp.bfloat16), "dp", axis=0, tiled=True),
        lax.all_gather(w_keyval.astype(jnp.bfloat16), "dp", axis=1, tiled=True),
        lax.all_gather(w_out.astype(jnp.bfloat16), "dp", axis=1, tiled=True),
        lax.all_gather(w_gateup.astype(jnp.bfloat16), "dp", axis=1, tiled=True),
        lax.all_gather(w_down.astype(jnp.bfloat16), "dp", axis=1, tiled=True),
    )
    gain_rows, query_weight, keyval_weight, out_weight, gateup_weight, down_weight = regathered
    gain_values = gain_rows.astype(jnp.float32)
    grad_down_weight = over_rows(hidden, cotangent)
    grad_hidden = against(cotangent, down_weight)
    gate_values = gateup[0]
    up_values = gateup[1]
    sigmoid_gate = jax.nn.sigmoid(gate_values)
    grad_gate = grad_hidden * up_values * sigmoid_gate * (1.0 + gate_values * (1.0 - sigmoid_gate))
    grad_up = grad_hidden * gate_values * sigmoid_gate
    grad_gateup = jnp.stack([grad_gate, grad_up]).astype(jnp.bfloat16)
    grad_gateup_weight = jnp.einsum(
        "nd,snf->sdf", normed_two, grad_gateup, preferred_element_type=jnp.float32
    )
    partial_two = jnp.einsum(
        "snf,sdf->nd", grad_gateup, gateup_weight, preferred_element_type=jnp.float32
    )
    grad_normed_two = lax.psum(partial_two, "tensor")
    grad_from_two, gain_grad_two = norm_back(grad_normed_two, unit_two, inverse_two, gain_values[1])
    grad_middle = cotangent.astype(jnp.float32) + grad_from_two
    grad_branch = grad_middle.astype(jnp.bfloat16)
    grad_out_weight = over_rows(mixture, grad_branch)
    grad_mixture = (
        against(grad_branch, out_weight)
        .astype(jnp.bfloat16)
        .reshape(length, local_groups, group_size, HD)
    )

    def backward_block(carried, pieces):
        start, logsum = pieces
        query_block, scaled = block_scores(start)
        soft_weights = jnp.exp(scaled - logsum[..., None])
        grad_block = lax.dynamic_slice_in_dim(grad_mixture, start, block_rows, 0)
        grad_soft = jnp.einsum(
            "qkgh,pkh->kgqp", grad_block, value_rows, preferred_element_type=jnp.float32
        )
        spread = jnp.sum(soft_weights * grad_soft, axis=-1, keepdims=True)
        grad_scores = (soft_weights * (grad_soft - spread) * inverse_scale).astype(jnp.bfloat16)
        grad_query = jnp.einsum(
            "kgqp,pkh->qkgh", grad_scores, key_rows, preferred_element_type=jnp.float32
        )
        grad_key = carried[0] + jnp.einsum(
            "kgqp,qkgh->pkh", grad_scores, query_block, preferred_element_type=jnp.float32
        )
        grad_value = carried[1] + jnp.einsum(
            "kgqp,qkgh->pkh",
            soft_weights.astype(jnp.bfloat16),
            grad_block,
            preferred_element_type=jnp.float32,
        )
        return ((grad_key, grad_value), grad_query)

    zero_rows = jnp.zeros((length, local_groups, HD), jnp.float32)
    (grad_keys, grad_values), grad_queries = lax.scan(
        backward_block, (zero_rows, zero_rows), (starts, logsum_blocks)
    )
    grad_queries = grad_queries.reshape(length, local_heads, HD)
    grad_query_raw = (
        unrotate(grad_queries, cosine_table, sine_table)
        .astype(jnp.bfloat16)
        .reshape(length, local_heads * HD)
    )
    grad_key_raw = unrotate(grad_keys, cosine_table, sine_table).reshape(length, local_groups * HD)
    grad_keyval = jnp.stack([grad_key_raw, grad_values.reshape(length, local_groups * HD)]).astype(
        jnp.bfloat16
    )
    grad_query_weight = over_rows(normed_one, grad_query_raw)
    grad_keyval_weight = jnp.einsum(
        "nd,snk->sdk", normed_one, grad_keyval, preferred_element_type=jnp.float32
    )
    partial_one = against(grad_query_raw, query_weight) + jnp.einsum(
        "snk,sdk->nd", grad_keyval, keyval_weight, preferred_element_type=jnp.float32
    )
    grad_normed_one = lax.psum(partial_one.astype(jnp.bfloat16), "tensor").astype(jnp.float32)
    grad_from_one, gain_grad_one = norm_back(grad_normed_one, unit_one, inverse_one, gain_values[0])
    input_grad = grad_middle + grad_from_one
    gain_grads = jnp.stack([gain_grad_one, gain_grad_two])
    reduced = (
        lax.psum_scatter(gain_grads, "dp", scatter_dimension=1, tiled=True),
        lax.psum_scatter(grad_query_weight, "dp", scatter_dimension=0, tiled=True),
        lax.psum_scatter(grad_keyval_weight, "dp", scatter_dimension=1, tiled=True),
        lax.psum_scatter(grad_out_weight, "dp", scatter_dimension=1, tiled=True),
        lax.psum_scatter(grad_gateup_weight, "dp", scatter_dimension=1, tiled=True),
        lax.psum_scatter(grad_down_weight, "dp", scatter_dimension=1, tiled=True),
    )
    first_owner = (lax.axis_index("tensor") == 0).astype(jnp.float32)
    local_square = first_owner * jnp.sum(reduced[0] * reduced[0]) + sum(
        (jnp.sum(g * g) for g in reduced[1:])
    )
    square_total = lax.psum(local_square, ("dp", "tensor"))
    grad_norm = jnp.sqrt(square_total)
    clip_factor = jnp.minimum(1.0, clip_limit / (grad_norm + 1e-06))
    step_float = step_count[0].astype(jnp.float32)
    params = (norm_gains, w_query, w_keyval, w_out, w_gateup, w_down)
    states = (
        (gains_first, gains_second),
        (query_first, query_second),
        (keyval_first, keyval_second),
        (out_first, out_second),
        (gateup_first, gateup_second),
        (down_first, down_second),
    )
    step_rates = (gain_rate, weight_rate, weight_rate, out_rate, weight_rate, weight_rate)
    decay_rates = (0.0, weight_decay, weight_decay, weight_decay, weight_decay, weight_decay)
    results = []
    for position_index in range(6):
        first, second = states[position_index]
        results.extend(
            adam_step(
                params[position_index],
                first,
                second,
                reduced[position_index],
                clip_factor,
                step_float,
                step_rates[position_index],
                decay_rates[position_index],
            )
        )
    return (
        layer_out,
        input_grad,
        grad_norm.reshape(1),
        results[0],
        results[1],
        results[2],
        results[3],
        results[4],
        results[5],
        results[6],
        results[7],
        results[8],
        results[9],
        results[10],
        results[11],
        results[12],
        results[13],
        results[14],
        results[15],
        results[16],
        results[17],
    )


def solution(mesh):
    in_specs = (
        P("dp", None),
        P("dp", None),
        P("dp", None),
        P(),
        P(None, "dp"),
        P(None, "dp"),
        P(None, "dp"),
        P("dp", "tensor"),
        P("dp", "tensor"),
        P("dp", "tensor"),
        P(None, "dp", "tensor"),
        P(None, "dp", "tensor"),
        P(None, "dp", "tensor"),
        P("tensor", "dp"),
        P("tensor", "dp"),
        P("tensor", "dp"),
        P(None, "dp", "tensor"),
        P(None, "dp", "tensor"),
        P(None, "dp", "tensor"),
        P("tensor", "dp"),
        P("tensor", "dp"),
        P("tensor", "dp"),
    )
    out_specs = (
        P("dp", None),
        P("dp", None),
        P(),
        P(None, "dp"),
        P(None, "dp"),
        P(None, "dp"),
        P("dp", "tensor"),
        P("dp", "tensor"),
        P("dp", "tensor"),
        P(None, "dp", "tensor"),
        P(None, "dp", "tensor"),
        P(None, "dp", "tensor"),
        P("tensor", "dp"),
        P("tensor", "dp"),
        P("tensor", "dp"),
        P(None, "dp", "tensor"),
        P(None, "dp", "tensor"),
        P(None, "dp", "tensor"),
        P("tensor", "dp"),
        P("tensor", "dp"),
        P("tensor", "dp"),
    )
    return jax.shard_map(
        on_device, mesh=mesh, in_specs=in_specs, out_specs=out_specs, check_vma=False
    )
```

profile of v0, /device:TPU:0, one launch (start us, length us, event | category | flops | bytes accessed | tf_op | source)
XLA Modules:
  0.0 1800.6 jit_solution(3728736641630619204)
XLA Ops:
  11.8 10.5 all_gather.24
  26.0 14.2 all_gather.26
  51.2 37.7 %while.28 = (s32[]{:T(128)}, bf16[2,512,512]{2,1,0:T(8,128)(2,1)}, f32[2,1,8,512]{3,2,1,0:T(8,128)}, s32[2]{0:T(128)S(1)}, s32[1024]{0:T(1024)S(1)}, /*index=5*/...) while((s32[]{:T(128)}, bf16[2,512,512]{2,1,0:T(8,128)(2,1)}, ...), condition=%wide.region_6.7_spmd.clone, body=%wide.region_3.6_spmd.clone.sunk | while | flops 1125904896 | bytes 64371432 | solution.py:165
  88.9 7.7 fusion.122
  100.9 287.2 %all-reduce.5.cloned.1.call-done = f32[1024,2048]{1,0:T(8,128)} async-done(((f32[1024,2048]{1,0:T(8,128)}), f32[1024,2048]{1,0:T(8,128)}) %all-reduce.5.cloned.1.call-update) | async-done | bytes 8388624 | tf_op jit(solution)/shard_map/psum | solution.py:168
  388.1 9.2 multiply_reduce_fusion.2
  397.4 59.8 %all-gather.9.cloned.1.call-done = bf16[2,2048,1408]{2,1,0:T(8,128)(2,1)} async-done(((bf16[2,256,1408]{2,1,0:T(8,128)(2,1)}), bf16[2,2048,1408]{2,1,0:T(8,128)(2,1)}) %all-gather.9.cloned.1.call-update) | async-done | bytes 11534352 | tf_op jit(solution)/shard_map/all_gather | solution.py:107
  457.2 20.2 %convolution_bitcast_fusion.3 = f32[2,1024,1408]{2,1,0:T(8,128)} fusion(bf16[2,2048,1408]{2,1,0:T(8,128)(2,1)} %all-gather.9.cloned.1.call-done, f32[1024,2048]{1,0:T(8,128)} %get-tuple-element.339, f32[2048]{0:T(1024)S(1)} %bitcast.364, f32[1024]{0:T(1024)S(1)} %add_rsqrt_fusion), kind=kOutput, calls=%fused_computation.85 | convolution fusion | flops 11817451520 | bytes 31469568 | tf_op jit(solution)/shard_map/nd,sdf->snf/dot_general | solution.py:173
  477.4 26.5 %all-gather.11.cloned.1.call-done = bf16[1408,2048]{1,0:T(8,128)(2,1)} async-done(((bf16[1408,256]{1,0:T(8,128)(2,1)}), bf16[1408,2048]{1,0:T(8,128)(2,1)}) %all-gather.11.cloned.1.call-update) | async-done | bytes 5767184 | tf_op jit(solution)/shard_map/all_gather | solution.py:108
  503.9 15.6 fusion.71
  522.0 17.0 convolution_bitcast_fusion.4
  539.1 11.3 convolution_convert_fusion
  550.4 279.6 %all-reduce.7.cloned.1.call-done = f32[1024,2048]{1,0:T(8,128)} async-done(((f32[1024,2048]{1,0:T(8,128)}), f32[1024,2048]{1,0:T(8,128)}) %all-reduce.7.cloned.1.call-update) | async-done | bytes 8388624 | tf_op jit(solution)/shard_map/psum | solution.py:206
  830.0 7.6 multiply_reduce_fusion
  850.9 129.5 %while.29 = (s32[]{:T(128)}, f32[1024,1,64]{0,2,1:T(8,128)}, f32[1024,1,64]{0,2,1:T(8,128)}, f32[2,512,1,8,64]{1,0,4,3,2:T(2,128)}, s32[2]{0:T(128)S(1)}, /*inde...) while((s32[]{:T(128)}, f32[1024,1,64]{0,2,1:T(8,128)}, ...), condition=%wide.region_14.15_spmd.clone, body=%wide.region_12.14_spmd.clone.sunk | while | flops 2728129024 | bytes 178878960 | solution.py:242
  859.7 10.8 fusion.181
  882.7 19.5 %dynamic_update_slice.22 = f32[2,512,1,8,64]{1,0,4,3,2:T(2,128)} dynamic-update-slice(f32[2,512,1,8,64]{1,0,4,3,2:T(2,128)} %get-tuple-element.553, f32[1,512,1,8,64]{1,0,4,3,2:T(1,128)S(1)} %copy.99, s32[]{:T(128)} %get-tuple-element.550, s32[]{:T(128)} %constant.54.clone.1..sunk.1, s32[]{:T(128)} %constant.54.clone.1..sunk.1, s32[]{:T(128)} %constant.54.clone.1..sunk.1, s32[]{:T(128)} %constant.54.clone.1..sunk.1) | dynamic-update-slice | bytes 2097156 | tf_op jit(solution)/shard_map/while/body/jit(dynamic_update_index_in_dim)/dynamic_update_slice | solution.py:242
  924.4 10.8 fusion.181
  947.4 19.5 %dynamic_update_slice.22 = f32[2,512,1,8,64]{1,0,4,3,2:T(2,128)} dynamic-update-slice(f32[2,512,1,8,64]{1,0,4,3,2:T(2,128)} %get-tuple-element.553, f32[1,512,1,8,64]{1,0,4,3,2:T(1,128)S(1)} %copy.99, s32[]{:T(128)} %get-tuple-element.550, s32[]{:T(128)} %constant.54.clone.1..sunk.1, s32[]{:T(128)} %constant.54.clone.1..sunk.1, s32[]{:T(128)} %constant.54.clone.1..sunk.1, s32[]{:T(128)} %constant.54.clone.1..sunk.1) | dynamic-update-slice | bytes 2097156 | tf_op jit(solution)/shard_map/while/body/jit(dynamic_update_index_in_dim)/dynamic_update_slice | solution.py:242
  972.1 7.6 fusion.184
  1008.6 7.8 fusion.78
  1016.5 269.4 %all-reduce.9.cloned.1.call-done = (bf16[1024,2048]{1,0:T(8,128)(2,1)}, bf16[1024,2048]{1,0:T(8,128)(2,1)}) async-done(((bf16[1024,2048]{1,0:T(8,128)(2,1)}, bf16[1024,2048]{1,0:T(8,128)(2,1)}), (bf16[1024,2048]{1,0:T(8,128)(2,1)}, bf16[1024,2048]{1,0:T(8,128)(2,1)})) %all-reduce.9.cloned.1.call-update) | async-done | bytes 8388624 | tf_op jit(solution)/shard_map/psum | solution.py:177
  1292.4 11.3 fusion.124
  1304.4 21.0 %convolution_bitcast_fusion.2 = f32[2,2048,1408]{1,2,0:T(8,128)} fusion(bf16[1,1024,1408]{2,1,0:T(8,128)(2,1)} %copy-done.62, bf16[1,1024,1408]{2,1,0:T(8,128)(2,1)} %copy-done.61, f32[1024,2048]{1,0:T(8,128)} %get-tuple-element.339, f32[2048]{0:T(1024)S(1)} %bitcast.367, f32[1024]{0:T(1024)S(1)} %copy-done.52), kind=kOutput, calls=%fused_computation.61 | convolution fusion | flops 11820335104 | bytes 37236736 | tf_op jit(solution)/shard_map/nd,snf->sdf/dot_general | solution.py:200
  1337.5 42.0 %reduce-scatter.9.cloned.1.call-done = f32[256,512]{1,0:T(8,128)} async-done(((f32[2048,512]{1,0:T(8,128)}), f32[256,512]{1,0:T(8,128)}) %reduce-scatter.9.cloned.1.call-update) | async-done | bytes 524304 | tf_op jit(solution)/shard_map/reduce_scatter | solution.py:268
  1382.5 51.9 %reduce-scatter.13.cloned.1.call-done = f32[512,256]{1,0:T(8,128)} async-done(((f32[512,2048]{1,0:T(8,128)}), f32[512,256]{1,0:T(8,128)}) %reduce-scatter.13.cloned.1.call-update) | async-done | bytes 524304 | tf_op jit(solution)/shard_map/reduce_scatter | solution.py:270
  1436.8 9.5 fusion.60
  1446.3 27.9 %reduce-scatter.19.cloned.1.call-done = f32[256,2]{1,0:T(8,128)} async-done(((f32[2048,2]{1,0:T(8,128)}), f32[256,2]{1,0:T(8,128)}) %reduce-scatter.19.cloned.1.call-update) | async-done | bytes 2064
  1476.4 87.9 %reduce-scatter.17.cloned.1.call-done = f32[1408,256]{1,0:T(8,128)} async-done(((f32[1408,2048]{1,0:T(8,128)}), f32[1408,256]{1,0:T(8,128)}) %reduce-scatter.17.cloned.1.call-update) | async-done | bytes 1441808 | tf_op jit(solution)/shard_map/reduce_scatter | solution.py:272
  1566.7 147.2 %reduce-scatter.15.cloned.1.call-done = f32[2,256,1408]{1,2,0:T(8,128)} async-done(((f32[2,2048,1408]{1,2,0:T(8,128)}), f32[2,256,1408]{1,2,0:T(8,128)}) %reduce-scatter.15.cloned.1.call-update) | async-done | bytes 2883600 | tf_op jit(solution)/shard_map/reduce_scatter | solution.py:271
  1718.4 8.4 add_convert_fusion
  1726.8 39.5 %psum.39 = f32[]{:T(128)} all-reduce(f32[]{:T(128)S(6)} %add.273), channel_id=1, replica_groups=mesh['dp'=8,'tensor'=4] {'dp','tensor'}, use_global_device_ids=true, to_apply=%region_31.32 | all-reduce | flops 1 | bytes 8 | tf_op jit(solution)/shard_map/psum | solution.py:278
  (292 shorter events, 211.2 us)
Async XLA Ops:
  7.2 18.8 %copy-start.37 = (f32[2,256,64]{1,2,0:T(8,128)S(1)}, f32[2,256,64]{1,2,0:T(8,128)}, u32[]{:S(2)}) copy-start(f32[2,256,64]{1,2,0:T(8,128)} %param.36) | copy-start | bytes 393220
  7.2 37.9 %all-gather.5.cloned.1.call-start = ((), (), s32[]{:S(2)}) async-start(), calls=%async_computation.6 | async-start | bytes 2359296 | tf_op jit(solution)/shard_map/all_gather | solution.py:104
  9.1 79.8 %all-gather.7.cloned.1.call-start = ((), (), s32[]{:S(2)}) async-start(), calls=%async_computation.7 | async-start | bytes 2359296 | tf_op jit(solution)/shard_map/all_gather | solution.py:106
  10.9 377.2 %all-reduce.5.cloned.1.call-start = ((), (), s32[]{:S(2)}) async-start(), calls=%async_computation.8 | async-start | bytes 16777216 | tf_op jit(solution)/shard_map/psum | solution.py:168
  11.0 29.3 %copy-start.2 = (bf16[1024,2048]{1,0:T(8,128)(2,1)S(1)}, bf16[1024,2048]{1,0:T(8,128)(2,1)}, u32[]{:S(2)}) copy-start(bf16[1024,2048]{1,0:T(8,128)(2,1)} %param.26) | copy-start | bytes 12582916
  22.9 22.1 %copy-start.47 = (f32[1,2048]{1,0:T(1,128)}, f32[1,2048]{1,0:T(1,128)S(1)}, u32[]{:S(2)}) copy-start(f32[1,2048]{1,0:T(1,128)S(1)} %get-tuple-element.356) | copy-start | bytes 24580
  26.0 19.0 %copy-start.53 = (f32[1024]{0:T(1024)}, f32[1024]{0:T(1024)S(1)}, u32[]{:S(2)}) copy-start(f32[1024]{0:T(1024)S(1)} %add_rsqrt_fusion.1) | copy-start | bytes 12292
  88.9 7.7 copy-start.17
  96.6 360.6 %all-gather.9.cloned.1.call-start = ((), (), s32[]{:S(2)}) async-start(), calls=%async_computation.9 | async-start | bytes 12976128 | tf_op jit(solution)/shard_map/all_gather | solution.py:107
  99.9 404.0 %all-gather.11.cloned.1.call-start = ((), (), s32[]{:S(2)}) async-start(), calls=%async_computation.10 | async-start | bytes 6488064 | tf_op jit(solution)/shard_map/all_gather | solution.py:108
  100.9 356.3 %copy-start.49 = (f32[1,2048]{1,0:T(1,128)S(1)}, f32[1,2048]{1,0:T(1,128)}, u32[]{:S(2)}) copy-start(f32[1,2048]{1,0:T(1,128)} %get-tuple-element.355) | copy-start | bytes 24580
  100.9 729.1 %all-reduce.7.cloned.1.call-start = ((), (), s32[]{:S(2)}) async-start(), calls=%async_computation.11 | async-start | bytes 16777216 | tf_op jit(solution)/shard_map/psum | solution.py:206
  397.4 440.3 %copy-start.51 = (f32[1024]{0:T(1024)}, f32[1024]{0:T(1024)S(1)}, u32[]{:S(2)}) copy-start(f32[1024]{0:T(1024)S(1)} %add_rsqrt_fusion) | copy-start | bytes 12292
  539.1 746.9 %all-reduce.9.cloned.1.call-start = ((), (), s32[]{:S(2)}) async-start(), calls=%async_computation.18 | async-start | bytes 16777216 | tf_op jit(solution)/shard_map/psum | solution.py:177
  830.0 8.2 copy-start.5
  830.0 9.4 copy-start.18
  839.5 8.1 copy-start.60
  881.6 20.6 %copy-start.7 = (f32[1024,1,64]{0,2,1:T(8,128)S(1)}, f32[1024,1,64]{0,2,1:T(8,128)}, u32[]{:S(2)}) copy-start(f32[1024,1,64]{0,2,1:T(8,128)} %get-tuple-element.551) | copy-start | bytes 786436 | tf_op jit(solution)/shard_map/while
  907.4 7.6 copy-start.8
  907.4 8.3 copy-start.4
  946.3 20.6 %copy-start.7 = (f32[1024,1,64]{0,2,1:T(8,128)S(1)}, f32[1024,1,64]{0,2,1:T(8,128)}, u32[]{:S(2)}) copy-start(f32[1024,1,64]{0,2,1:T(8,128)} %get-tuple-element.551) | copy-start | bytes 786436 | tf_op jit(solution)/shard_map/while
  972.1 7.6 copy-start.8
  972.1 8.3 copy-start.4
  995.2 340.7 %reduce-scatter.11.cloned.1.call-start = ((), (), s32[]{:S(2)}) async-start(), calls=%async_computation.13 | async-start | bytes 1179648 | tf_op jit(solution)/shard_map/reduce_scatter | solution.py:269
  1000.5 379.0 %reduce-scatter.9.cloned.1.call-start = ((), (), s32[]{:S(2)}) async-start(), calls=%async_computation.12 | async-start | bytes 4718592 | tf_op jit(solution)/shard_map/reduce_scatter | solution.py:268
  1007.4 427.0 %reduce-scatter.13.cloned.1.call-start = ((), (), s32[]{:S(2)}) async-start(), calls=%async_computation.14 | async-start | bytes 4718592 | tf_op jit(solution)/shard_map/reduce_scatter | solution.py:270
  1016.5 457.7 %reduce-scatter.19.cloned.1.call-start = ((), (), s32[]{:S(2)}) async-start(), calls=%async_computation.17 | async-start | bytes 1179648
  1292.3 272.0 %reduce-scatter.17.cloned.1.call-start = ((), (), s32[]{:S(2)}) async-start(), calls=%async_computation.16 | async-start | bytes 12976128 | tf_op jit(solution)/shard_map/reduce_scatter | solution.py:272
  1303.8 410.1 %reduce-scatter.15.cloned.1.call-start = ((), (), s32[]{:S(2)}) async-start(), calls=%async_computation.15 | async-start | bytes 25952256 | tf_op jit(solution)/shard_map/reduce_scatter | solution.py:271
  1718.4 48.7 %copy-start.10 = (f32[2,256,1408]{1,2,0:T(8,128)S(1)}, f32[2,256,1408]{1,2,0:T(8,128)}, u32[]{:S(2)}) copy-start(f32[2,256,1408]{1,2,0:T(8,128)} %reduce-scatter.15.cloned.1.call-done) | copy-start | bytes 8650756
  1783.2 7.1 copy-start.38
  1783.2 7.0 copy-start.39
  (55 other events, 178.7 us)
Sparse Core Ops, SparseCore 0:
  10.5 32.9 all-gather.4
  45.9 28.5 all-gather.6
  96.7 291.3 all-reduce.4
  390.5 66.6 all-gather.8
  459.5 44.3 all-gather.10
  539.2 290.8 all-reduce.6
  995.4 290.5 all-reduce.8
  1289.7 35.0 reduce-scatter.10
  1328.1 51.2 reduce-scatter.8
  1383.0 51.3 reduce-scatter.12
  1438.2 35.9 reduce-scatter.18
  1477.5 86.7 reduce-scatter.16
  1568.0 145.8 reduce-scatter.14
where the time goes:
time: 1810 us; the launch traced here: 1800 us
  waiting for transfers between devices  1280 us (71%)
  matrix products  218 us (12%)
  other arithmetic  120 us (7%)
  local copies, waits for them, and re-layouts  87.9 us (5%)
  blocking collectives  64.2 us (4%)
  between operations  22.3 us (1%)
    psum x1, waiting for transfers between devices, on_device(): branch = lax.psum(branch_partial, 'tensor')  287 us
    psum x1, waiting for transfers between devices, on_device(): grad_normed_two = lax.psum(partial_two, 'tensor')  280 us
    psum x1, waiting for transfers between devices, on_device(): lax.psum(jnp.dot(hidden, down_weight, preferred_element_type=jnp.float32)...  269 us
    reduce_scatter x1, waiting for transfers between devices, on_device(): lax.psum_scatter(grad_gateup_weight, 'dp', scatter_dimension=1, tiled=True)  147 us
    reduce_scatter x1, waiting for transfers between devices, on_device(): lax.psum_scatter(grad_down_weight, 'dp', scatter_dimension=1, tiled=True)  87.9 us
    all_gather x1, waiting for transfers between devices, on_device(): lax.all_gather(w_gateup.astype(jnp.bfloat16), 'dp', axis=1, tiled=True)  59.8 us
    reduce_scatter x1, waiting for transfers between devices, on_device(): lax.psum_scatter(grad_out_weight, 'dp', scatter_dimension=1, tiled=True)  51.9 us
    reduce_scatter x1, waiting for transfers between devices, on_device(): lax.psum_scatter(grad_query_weight, 'dp', scatter_dimension=0, tiled=True)  42 us
  transfers between devices with their start and end apart: 13, of which 10 were waited for; matrix products, arithmetic and copies ran while one was open for 10% of the time, Pallas kernels for 0%

commit v1 on v0

--- a/solution.py
+++ b/solution.py
@@ -165,7 +165,9 @@
     mixed_blocks, logsum_blocks = lax.map(forward_block, starts)
     mixture = mixed_blocks.reshape(length, local_heads * HD)
     branch_partial = jnp.dot(mixture, out_weight, preferred_element_type=jnp.float32)
-    branch = lax.psum(branch_partial, "tensor")
+    branch = branch_partial
+    for hop in (1, 2):
+        branch = branch + lax.ppermute(branch, "tensor", [(dev, dev ^ hop) for dev in range(4)])
     middle = values_in + branch
     inverse_two = lax.rsqrt(jnp.mean(middle * middle, axis=-1, keepdims=True) + norm_eps)
     unit_two = middle * inverse_two

time: 1810 us -> 1990 us (1.099)
  waiting for transfers between devices: 1280 us -> 1450 us
    ppermute x0 -> x2, waiting for transfers between devices: none -> 541 us  [on_device(): lax.ppermute(branch, 'tensor', [(dev, dev ^ hop) for dev in range(4)])]
    psum x1 -> x0, waiting for transfers between devices: 287 us -> none  [on_device(): branch = lax.psum(branch_partial, 'tensor')]
    all_gather x1, waiting for transfers between devices: 59.8 us -> 0.02 us  [on_device(): lax.all_gather(w_gateup.astype(jnp.bfloat16), 'dp', axis=1, tiled=True)]
    all_gather x1, waiting for transfers between devices: 26.5 us -> 0.01 us  [on_device(): lax.all_gather(w_down.astype(jnp.bfloat16), 'dp', axis=1, tiled=True)]
  transfers between devices with their start and end apart: 13 -> 14, of which waited for: 10 -> 9; matrix products, arithmetic and copies ran while one was open for 10% -> 10% of each run, Pallas kernels for 0% -> 0%
where the time goes in v1:
time: 1990 us; the launch traced here: 1980 us
  waiting for transfers between devices  1450 us (73%)
  matrix products  218 us (11%)
  other arithmetic  131 us (7%)
  local copies, waits for them, and re-layouts  86.4 us (4%)
  blocking collectives  64.8 us (3%)
  between operations  22.6 us (1%)
    ppermute x2, waiting for transfers between devices, on_device(): lax.ppermute(branch, 'tensor', [(dev, dev ^ hop) for dev in range(4)])  541 us
    psum x1, waiting for transfers between devices, on_device(): grad_normed_two = lax.psum(partial_two, 'tensor')  280 us
    psum x1, waiting for transfers between devices, on_device(): lax.psum(jnp.dot(hidden, down_weight, preferred_element_type=jnp.float32)...  269 us
    reduce_scatter x1, waiting for transfers between devices, on_device(): lax.psum_scatter(grad_gateup_weight, 'dp', scatter_dimension=1, tiled=True)  147 us
    reduce_scatter x1, waiting for transfers between devices, on_device(): lax.psum_scatter(grad_down_weight, 'dp', scatter_dimension=1, tiled=True)  88.1 us
    reduce_scatter x1, waiting for transfers between devices, on_device(): lax.psum_scatter(grad_out_weight, 'dp', scatter_dimension=1, tiled=True)  52 us
    reduce_scatter x1, waiting for transfers between devices, on_device(): lax.psum_scatter(grad_query_weight, 'dp', scatter_dimension=0, tiled=True)  42.1 us
    dynamic_update_slice x4, local copies, waits for them, and re-layouts, on_device(): lax.scan(backward_block, (zero_rows, zero_rows), (starts, logsum_blocks))  41.2 us
  transfers between devices with their start and end apart: 14, of which 9 were waited for; matrix products, arithmetic and copies ran while one was open for 10% of the time, Pallas kernels for 0%

profile of v1, /device:TPU:0, one launch (start us, length us, event | category | flops | bytes accessed | tf_op | source)
XLA Modules:
  0.0 1983.5 jit_solution(13096602555428225069)
XLA Ops:
  14.1 10.6 all_gather.24
  28.5 14.7 all_gather.26
  54.8 37.3 %while.28 = (s32[]{:T(128)}, bf16[2,512,512]{2,1,0:T(8,128)(2,1)S(1)}, f32[2,1,8,512]{3,2,1,0:T(8,128)}, s32[2]{0:T(128)S(1)}, s32[1024]{0:T(1024)S(1)}, /*index...) while((s32[]{:T(128)}, ...), condition=%wide.region_6.7_spmd.clone, body=%wide.region_3.6_spmd.clone.sunk | while | flops 1125904896 | bytes 55982772 | solution.py:165
  101.3 181.3 %collective-permute-done = f32[1024,2048]{1,0:T(8,128)} collective-permute-done((f32[1024,2048]{1,0:T(8,128)S(1)}, f32[1024,2048]{1,0:T(8,128)}, u32[]{:S(2)}, u32[]{:S(2)}) %collective-permute-start) | collective-permute-done | bytes 8388640 | tf_op jit(solution)/shard_map/ppermute | solution.py:170
  282.6 11.9 add.263
  297.9 359.4 %collective-permute-done.1 = f32[1024,2048]{1,0:T(8,128)} collective-permute-done((f32[1024,2048]{1,0:T(8,128)}, f32[1024,2048]{1,0:T(8,128)}, u32[]{:S(2)}, u32[]{:S(2)}) %collective-permute-start.1) | collective-permute-done | bytes 8388640 | tf_op jit(solution)/shard_map/ppermute | solution.py:170
  657.4 12.0 multiply_reduce_fusion.2
  669.5 20.0 %convolution_bitcast_fusion.3 = f32[2,1024,1408]{2,1,0:T(8,128)} fusion(bf16[2,2048,1408]{2,1,0:T(8,128)(2,1)} %all-gather.9.cloned.1.call-done, f32[1024,2048]{1,0:T(8,128)} %get-tuple-element.339, f32[2048]{0:T(1024)S(1)} %bitcast.364, f32[1024]{0:T(1024)S(1)} %add_rsqrt_fusion), kind=kOutput, calls=%fused_computation.85 | convolution fusion | flops 11817451520 | bytes 31469568 | tf_op jit(solution)/shard_map/nd,sdf->snf/dot_general | solution.py:175
  689.5 15.6 fusion.71
  707.7 17.1 convolution_bitcast_fusion.4
  724.9 10.9 convolution_convert_fusion
  735.8 280.0 %all-reduce.4.cloned.1.call-done = f32[1024,2048]{1,0:T(8,128)} async-done(((f32[1024,2048]{1,0:T(8,128)}), f32[1024,2048]{1,0:T(8,128)}) %all-reduce.4.cloned.1.call-update) | async-done | bytes 8388624 | tf_op jit(solution)/shard_map/psum | solution.py:208
  1015.8 7.6 multiply_reduce_fusion
  1033.7 130.4 %while.29 = (s32[]{:T(128)}, f32[1024,1,64]{0,2,1:T(8,128)S(1)}, f32[1024,1,64]{0,2,1:T(8,128)S(1)}, f32[2,512,1,8,64]{1,0,4,3,2:T(2,128)}, s32[2]{0:T(128)S(1)}...) while((s32[]{:T(128)}, f32[1024,1,64]{0,2,1:T(8,128)S(1)}, ...), condition=%wide.region_13.14_spmd.clone, body=%wide.region_11.13_spmd.clone.sunk | while | flops 2728129024 | bytes 182942096 | solution.py:244
  1043.0 11.5 fusion.181
  1066.6 19.5 dynamic_update_slice.22
  1091.5 7.5 fusion.184
  1107.9 11.5 fusion.181
  1131.6 19.5 dynamic_update_slice.22
  1156.4 7.5 fusion.184
  1191.2 7.8 fusion.78
  1199.1 269.4 %all-reduce.6.cloned.1.call-done = (bf16[1024,2048]{1,0:T(8,128)(2,1)}, bf16[1024,2048]{1,0:T(8,128)(2,1)}) async-done(((bf16[1024,2048]{1,0:T(8,128)(2,1)}, bf16[1024,2048]{1,0:T(8,128)(2,1)}), (bf16[1024,2048]{1,0:T(8,128)(2,1)}, bf16[1024,2048]{1,0:T(8,128)(2,1)})) %all-reduce.6.cloned.1.call-update) | async-done | bytes 8388624 | tf_op jit(solution)/shard_map/psum | solution.py:179
  1475.0 11.4 fusion.124
  1487.1 20.8 %convolution_bitcast_fusion.2 = f32[2,2048,1408]{1,2,0:T(8,128)} fusion(bf16[1,1024,1408]{2,1,0:T(8,128)(2,1)} %copy-done.58, bf16[1,1024,1408]{2,1,0:T(8,128)(2,1)} %copy-done.57, f32[1024,2048]{1,0:T(8,128)} %get-tuple-element.339, f32[2048]{0:T(1024)S(1)} %bitcast.367, f32[1024]{0:T(1024)S(1)} %copy-done.47), kind=kOutput, calls=%fused_computation.61 | convolution fusion | flops 11820335104 | bytes 37236736 | tf_op jit(solution)/shard_map/nd,snf->sdf/dot_general | solution.py:202
  1520.0 42.1 %reduce-scatter.9.cloned.1.call-done = f32[256,512]{1,0:T(8,128)} async-done(((f32[2048,512]{1,0:T(8,128)}), f32[256,512]{1,0:T(8,128)}) %reduce-scatter.9.cloned.1.call-update) | async-done | bytes 524304 | tf_op jit(solution)/shard_map/reduce_scatter | solution.py:270
  1565.1 52.0 %reduce-scatter.13.cloned.1.call-done = f32[512,256]{1,0:T(8,128)} async-done(((f32[512,2048]{1,0:T(8,128)}), f32[512,256]{1,0:T(8,128)}) %reduce-scatter.13.cloned.1.call-update) | async-done | bytes 524304 | tf_op jit(solution)/shard_map/reduce_scatter | solution.py:272
  1619.6 9.5 fusion.60
  1629.1 27.7 %reduce-scatter.19.cloned.1.call-done = f32[256,2]{1,0:T(8,128)} async-done(((f32[2048,2]{1,0:T(8,128)}), f32[256,2]{1,0:T(8,128)}) %reduce-scatter.19.cloned.1.call-update) | async-done | bytes 2064
  1659.0 88.1 %reduce-scatter.17.cloned.1.call-done = f32[1408,256]{1,0:T(8,128)} async-done(((f32[1408,2048]{1,0:T(8,128)}), f32[1408,256]{1,0:T(8,128)}) %reduce-scatter.17.cloned.1.call-update) | async-done | bytes 1441808 | tf_op jit(solution)/shard_map/reduce_scatter | solution.py:274
  1749.4 147.1 %reduce-scatter.15.cloned.1.call-done = f32[2,256,1408]{1,2,0:T(8,128)} async-done(((f32[2,2048,1408]{1,2,0:T(8,128)}), f32[2,256,1408]{1,2,0:T(8,128)}) %reduce-scatter.15.cloned.1.call-update) | async-done | bytes 2883600 | tf_op jit(solution)/shard_map/reduce_scatter | solution.py:273
  1901.0 8.4 add_convert_fusion
  1909.4 39.5 %psum.31 = f32[]{:T(128)} all-reduce(f32[]{:T(128)S(6)} %add.279), channel_id=1, replica_groups=mesh['dp'=8,'tensor'=4] {'dp','tensor'}, use_global_device_ids=true, to_apply=%region_30.31 | all-reduce | flops 1 | bytes 8 | tf_op jit(solution)/shard_map/psum | solution.py:280
  (276 shorter events, 209.7 us)
Async XLA Ops:
  7.2 41.4 %all-gather.5.cloned.1.call-start = ((), (), s32[]{:S(2)}) async-start(), calls=%async_computation.6 | async-start | bytes 2359296 | tf_op jit(solution)/shard_map/all_gather | solution.py:104
  9.1 83.0 %all-gather.7.cloned.1.call-start = ((), (), s32[]{:S(2)}) async-start(), calls=%async_computation.7 | async-start | bytes 2359296 | tf_op jit(solution)/shard_map/all_gather | solution.py:106
  10.9 17.6 copy-start.33
  10.9 658.5 %all-gather.9.cloned.1.call-start = ((), (), s32[]{:S(2)}) async-start(), calls=%async_computation.8 | async-start | bytes 12976128 | tf_op jit(solution)/shard_map/all_gather | solution.py:107
  14.0 675.5 %all-gather.11.cloned.1.call-start = ((), (), s32[]{:S(2)}) async-start(), calls=%async_computation.9 | async-start | bytes 6488064 | tf_op jit(solution)/shard_map/all_gather | solution.py:108
  14.1 29.1 %copy-start.4 = (bf16[1024,2048]{1,0:T(8,128)(2,1)S(1)}, bf16[1024,2048]{1,0:T(8,128)(2,1)}, u32[]{:S(2)}) copy-start(bf16[1024,2048]{1,0:T(8,128)(2,1)} %param.26) | copy-start | bytes 12582916
  25.4 23.3 %copy-start.42 = (f32[1,2048]{1,0:T(1,128)}, f32[1,2048]{1,0:T(1,128)S(1)}, u32[]{:S(2)}) copy-start(f32[1,2048]{1,0:T(1,128)S(1)} %get-tuple-element.356) | copy-start | bytes 24580
  28.5 20.2 %copy-start.48 = (f32[1024]{0:T(1024)}, f32[1024]{0:T(1024)S(1)}, u32[]{:S(2)}) copy-start(f32[1024]{0:T(1024)S(1)} %add_rsqrt_fusion.1) | copy-start | bytes 12292
  99.8 197.1 %copy-start.14 = (f32[1408,256]{1,0:T(8,128)S(1)}, f32[1408,256]{1,0:T(8,128)}, u32[]{:S(2)}) copy-start(f32[1408,256]{1,0:T(8,128)} %param.45) | copy-start | bytes 4325380
  99.8 182.8 %collective-permute-start = (f32[1024,2048]{1,0:T(8,128)S(1)}, f32[1024,2048]{1,0:T(8,128)}, u32[]{:S(2)}, u32[]{:S(2)}) collective-permute-start(f32[1024,2048]{1,0:T(8,128)S(1)} %fusion.122), channel_id=1, source_target_pairs={{0,1},{1,0},{2,3},{3,2},{4,5},{5,4},{6,7},{7,6},{8,9},{9,8},{10,11... | collective-permute-start | bytes 25165832 | tf_op jit(solution)/shard_map/ppermute | solution.py:170
  294.5 362.9 %collective-permute-start.1 = (f32[1024,2048]{1,0:T(8,128)}, f32[1024,2048]{1,0:T(8,128)}, u32[]{:S(2)}, u32[]{:S(2)}) collective-permute-start(f32[1024,2048]{1,0:T(8,128)} %add.263), channel_id=1, source_target_pairs={{0,2},{1,3},{2,0},{3,1},{4,6},{5,7},{6,4},{7,5},{8,10},{9,11},{10,... | collective-permute-start | bytes 25165832 | tf_op jit(solution)/shard_map/ppermute | solution.py:170
  297.9 371.6 %copy-start.44 = (f32[1,2048]{1,0:T(1,128)S(1)}, f32[1,2048]{1,0:T(1,128)}, u32[]{:S(2)}) copy-start(f32[1,2048]{1,0:T(1,128)} %get-tuple-element.355) | copy-start | bytes 24580
  297.9 717.9 %all-reduce.4.cloned.1.call-start = ((), (), s32[]{:S(2)}) async-start(), calls=%async_computation.10 | async-start | bytes 16777216 | tf_op jit(solution)/shard_map/psum | solution.py:208
  669.4 354.0 %copy-start.46 = (f32[1024]{0:T(1024)}, f32[1024]{0:T(1024)S(1)}, u32[]{:S(2)}) copy-start(f32[1024]{0:T(1024)S(1)} %add_rsqrt_fusion) | copy-start | bytes 12292
  724.8 743.7 %all-reduce.6.cloned.1.call-start = ((), (), s32[]{:S(2)}) async-start(), calls=%async_computation.17 | async-start | bytes 16777216 | tf_op jit(solution)/shard_map/psum | solution.py:179
  1015.8 8.2 copy-start.7
  1015.8 9.4 copy-start.15
  1091.5 7.6 copy-start.2
  1091.5 7.6 copy-start.6
  1156.4 7.6 copy-start.2
  1156.4 7.6 copy-start.6
  1177.8 340.6 %reduce-scatter.11.cloned.1.call-start = ((), (), s32[]{:S(2)}) async-start(), calls=%async_computation.12 | async-start | bytes 1179648 | tf_op jit(solution)/shard_map/reduce_scatter | solution.py:271
  1183.1 379.0 %reduce-scatter.9.cloned.1.call-start = ((), (), s32[]{:S(2)}) async-start(), calls=%async_computation.11 | async-start | bytes 4718592 | tf_op jit(solution)/shard_map/reduce_scatter | solution.py:270
  1190.0 427.1 %reduce-scatter.13.cloned.1.call-start = ((), (), s32[]{:S(2)}) async-start(), calls=%async_computation.13 | async-start | bytes 4718592 | tf_op jit(solution)/shard_map/reduce_scatter | solution.py:272
  1199.1 457.7 %reduce-scatter.19.cloned.1.call-start = ((), (), s32[]{:S(2)}) async-start(), calls=%async_computation.16 | async-start | bytes 1179648
  1474.9 272.1 %reduce-scatter.17.cloned.1.call-start = ((), (), s32[]{:S(2)}) async-start(), calls=%async_computation.15 | async-start | bytes 12976128 | tf_op jit(solution)/shard_map/reduce_scatter | solution.py:274
  1486.4 410.1 %reduce-scatter.15.cloned.1.call-start = ((), (), s32[]{:S(2)}) async-start(), calls=%async_computation.14 | async-start | bytes 25952256 | tf_op jit(solution)/shard_map/reduce_scatter | solution.py:273
  1901.0 48.7 %copy-start.9 = (f32[2,256,1408]{1,2,0:T(8,128)S(1)}, f32[2,256,1408]{1,2,0:T(8,128)}, u32[]{:S(2)}) copy-start(f32[2,256,1408]{1,2,0:T(8,128)} %reduce-scatter.15.cloned.1.call-done) | copy-start | bytes 8650756
  1965.8 7.1 copy-start.34
  1965.8 7.0 copy-start.35
  1965.8 7.0 copy-start.40
  1965.8 7.0 copy-start.41
  (47 other events, 153.6 us)
Sparse Core Ops, SparseCore 0:
  10.5 33.1 all-gather.4
  46.2 28.3 all-gather.6
  77.0 67.6 all-gather.8
  298.0 42.5 all-gather.10
  725.0 290.8 all-reduce.3
  1177.9 290.5 all-reduce.5
  1472.3 35.0 reduce-scatter.10
  1510.7 51.2 reduce-scatter.8
  1565.8 51.3 reduce-scatter.12
  1620.7 35.9 reduce-scatter.18
  1660.3 86.7 reduce-scatter.16
  1750.5 145.9 reduce-scatter.14
